TPU v7x, 32 devices: a whole 2x2x4 slice. The times are simulated.
32 devices in a mesh: seq: 8 (over z, x), tp: 4 (over y, core).
Axes of the slice: x: 2, y: 2, z: 4, core: 2. Of those that a mesh axis runs over, the one named last changes fastest.
Arguments:
- conv_in: bfloat16 [1024, 16384], P('seq', 'tp'), may hold values from -6 to 6
- conv_weight: float32 [4, 16384], P(None, 'tp'), may hold values from -3 to 3
- conv_bias: float32 [16384], P('tp'), may hold values from -0.5 to 0.5
- proj_weight: bfloat16 [16384, 544], P('tp'), may hold values from -0.046875 to 0.046875
- dt_weight: bfloat16 [512, 16384], P(None, 'tp'), may hold values from -0.25 to 0.25
- dt_bias: float32 [16384], P('tp'), may hold values from -6 to -2.5
- decay_rate: float32 [16, 16384], P(None, 'tp'), may hold values from 0.0009765625 to 4
- skip_gain: float32 [16384], P('tp'), may hold values from 0.5 to 1.5
- grad_out: bfloat16 [1024, 16384], P('seq', 'tp'), may hold values from -6 to 6
Outputs:
- mixed: bfloat16 [1024, 16384], P('seq', 'tp')
- weight_grad: float32 [4, 4096, 16], P('tp', 'seq')
All inputs are finite; a program needn't handle non-finite values.
Results may differ from a plain program's by a relative error of at most 0.006.
Values may be sent and summed in bfloat16 or wider, within the bound.
No kernel may reach another device: no remote copies, remote signals or barrier semaphores. Data moves between devices by JAX's collectives and lax.ppermute only.
A program may use at most 128 MiB of HBM per device.

v0:
```python
import jax
import jax.numpy as jnp
from jax import lax
from jax.sharding import PartitionSpec as P

block_len = 16


def shifted(shard, axis, by):
    count = lax.axis_size(axis)
    pairs = [(i, i + by) for i in range(count) if 0 <= i + by < count]
    return lax.ppermute(shard, axis, pairs)


def entering(part, axis, combine, identity):
    place = lax.axis_index(axis)
    gathered = jax.tree.map(lambda a: lax.all_gather(a, axis), part)
    state = jax.tree.map(lambda a, e: jnp.zeros_like(a) + jnp.asarray(e, a.dtype), part, identity)

    def one(turn, state):
        return combine(
            state, jax.tree.map(lambda a: lax.dynamic_index_in_dim(a, turn, 0, False), gathered)
        )

    return lax.fori_loop(0, place, one, state)


def chain_pair(earlier, later):
    return (earlier[0] * later[0], later[0] * earlier[1] + later[1])


def local_pass(initial, decay_rate, slices):

    def block_step(carried, pieces):
        step_now, drive_now, b_now, c_now, grad_now = pieces
        outputs = []
        grads = []
        for offset in range(block_len):
            carried = (
                jnp.exp(-step_now[offset][None, :] * decay_rate) * carried
                + drive_now[offset][None, :] * b_now[offset][:, None]
            )
            outputs.append(jnp.sum(carried * c_now[offset][:, None], axis=0))
            grads.append(jnp.sum(carried * grad_now[offset][None, :], axis=1))
        return (carried, (jnp.stack(outputs), jnp.stack(grads)))

    return lax.scan(block_step, initial, slices)


def local_ending(step_size, drive_in, b_matrix, decay_rate):
    after = jnp.flip(jnp.cumsum(jnp.flip(step_size, 0), axis=0), 0) - step_size
    rows = []
    for state_index in range(decay_rate.shape[0]):
        weights = jnp.exp(-decay_rate[state_index][None, :] * after)
        rows.append(
            jnp.sum(weights * drive_in * b_matrix[:, state_index : state_index + 1], axis=0)
        )
    return jnp.stack(rows)


def on_device(
    conv_in,
    conv_weight,
    conv_bias,
    proj_weight,
    dt_weight,
    dt_bias,
    decay_rate,
    skip_gain,
    grad_out,
):
    tok_rows, channels = conv_in.shape
    taps = conv_weight.shape[0]
    rank_width = dt_weight.shape[0]
    states = decay_rate.shape[0]
    tok_total = tok_rows * lax.axis_size("seq")
    rim_rows = shifted(conv_in[tok_rows - (taps - 1) :], "seq", 1)
    extended = jnp.concatenate([rim_rows, conv_in], axis=0).astype(jnp.float32)
    pre_act = conv_bias[None, :] + jnp.zeros((tok_rows, channels), jnp.float32)
    for tap_index in range(taps):
        pre_act = (
            pre_act + conv_weight[tap_index][None, :] * extended[tap_index : tap_index + tok_rows]
        )
    conv_out = jax.nn.silu(pre_act).astype(jnp.bfloat16)
    partial_proj = jnp.dot(conv_out, proj_weight, preferred_element_type=jnp.float32)
    proj_out = lax.psum(partial_proj, "tp").astype(jnp.bfloat16)
    dt_low = proj_out[:, :rank_width]
    b_matrix = proj_out[:, rank_width : rank_width + states].astype(jnp.float32)
    c_matrix = proj_out[:, rank_width + states :].astype(jnp.float32)
    step_size = jax.nn.softplus(
        jnp.dot(dt_low, dt_weight, preferred_element_type=jnp.float32) + dt_bias[None, :]
    )
    drive_in = step_size * conv_out.astype(jnp.float32)
    scaled_grad = grad_out.astype(jnp.float32) / tok_total
    blocks = tok_rows // block_len
    slices = (
        step_size.reshape(blocks, block_len, channels),
        drive_in.reshape(blocks, block_len, channels),
        b_matrix.reshape(blocks, block_len, states),
        c_matrix.reshape(blocks, block_len, states),
        scaled_grad.reshape(blocks, block_len, channels),
    )
    zero_state = jnp.zeros((states, channels), jnp.float32)
    local_end = local_ending(step_size, drive_in, b_matrix, decay_rate)
    total_decay = jnp.exp(-decay_rate * jnp.sum(step_size, axis=0)[None, :])
    identity = (jnp.ones((states, channels), jnp.float32), zero_state)
    _, incoming = entering((total_decay, local_end), "seq", chain_pair, identity)
    _, (scan_out, grad_parts) = local_pass(incoming, decay_rate, slices)
    mixed = (
        scan_out.reshape(tok_rows, channels) + skip_gain[None, :] * conv_out.astype(jnp.float32)
    ).astype(jnp.bfloat16)
    grad_c = lax.psum(grad_parts.reshape(tok_rows, states), "tp").astype(jnp.bfloat16)
    weight_grad = lax.psum_scatter(
        lax.dot_general(
            conv_out, grad_c, (((0,), (0,)), ((), ())), preferred_element_type=jnp.float32
        ),
        "seq",
        scatter_dimension=0,
        tiled=True,
    )
    return (mixed, weight_grad[None])


def solution(mesh):
    return jax.shard_map(
        on_device,
        mesh=mesh,
        in_specs=(
            P("seq", "tp"),
            P(None, "tp"),
            P("tp"),
            P("tp", None),
            P(None, "tp"),
            P("tp"),
            P(None, "tp"),
            P("tp"),
            P("seq", "tp"),
        ),
        out_specs=(P("seq", "tp"), P("tp", "seq", None)),
        check_vma=False,
    )
```

profile of v0, /device:TPU:0, one launch (start us, length us, event | category | flops | bytes accessed | tf_op | source)
XLA Modules:
  0.0 394.6 jit_solution(8271281646402718323)
XLA Ops:
  8.1 4.9 %collective-permute-start = (bf16[3,4096]{1,0:T(4,128)(2,1)S(1)}, bf16[3,4096]{1,0:T(4,128)(2,1)S(1)}, u32[]{:S(2)}, u32[]{:S(2)}) collective-permute-start(bf16[3,4096]{1,0:T(4,128)(2,1)S(1)} %slice.453), channel_id=1, source_target_pairs={{0,4},{4,8},{8,12},{12,16},{16,20},{20,24},{24,28},{1,5},{5,9},{9,... | collective-permute-start | bytes 73736 | tf_op jit(solution)/shard_map/ppermute | solution.py:12
  21.9 14.5 %all-reduce.1 = bf16[128,544]{0,1:T(8,128)(2,1)S(1)} all-reduce(f32[128,544]{0,1:T(8,128)S(1)} %fusion.59), channel_id=1, replica_groups=mesh['seq'=8,'tp'=4] {'tp'}, use_global_device_ids=true, to_apply=%region_0.1 | all-reduce | flops 69632 | bytes 417792 | tf_op jit(solution)/shard_map/psum | solution.py:86
  37.0 6.0 %fusion.58 = (f32[4096]{0:T(1024)}, f32[128,4096]{1,0:T(8,128)}) fusion(f32[4096]{0:T(1024)S(1)} %copy-done.14, bf16[512,4096]{1,0:T(8,128)(2,1)} %param.17, bf16[128,544]{0,1:T(8,128)(2,1)S(1)} %all-reduce.1), kind=kOutput, calls=%fused_computation.252 | convolution fusion | flops 541061120 | bytes 6455296 | tf_op jit(solution)/shard_map/dot_general | solution.py:91
  43.0 16.6 %rev.7 = f32[128,4096]{1,0:T(8,128)} reverse(f32[128,4096]{1,0:T(8,128)} %get-tuple-element.359), dimensions={0} | reverse | bytes 4194304 | tf_op jit(solution)/shard_map/jit(_flip)/rev | solution.py:51
  59.6 4.6 %reduce_window_sum.11 = f32[128,4096]{1,0:T(8,128)} reduce-window(f32[128,4096]{1,0:T(8,128)} %rev.7, f32[]{:T(128)} %constant.51.clone.1), window={size=128x1 pad=127_0x0_0}, to_apply=%region_2.3 | reduce-window | flops 66584576 | bytes 4194308 | tf_op jit(solution)/shard_map/jit(cumsum)/reduce_window_sum | solution.py:51
  64.2 16.6 %rev.8 = f32[128,4096]{1,0:T(8,128)} reverse(f32[128,4096]{1,0:T(8,128)} %reduce_window_sum.11), dimensions={0} | reverse | bytes 4194304 | tf_op jit(solution)/shard_map/jit(_flip)/rev | solution.py:51
  80.8 7.7 %multiply_reduce_fusion.32 = (f32[4096]{0:T(1024)}, f32[4096]{0:T(1024)}, f32[4096]{0:T(1024)}, f32[4096]{0:T(1024)}, f32[4096]{0:T(1024)}, /*index=5*/f32[4096]...) fusion(f32[128]{0:T(128)S(1)} %get-tuple-element.343, ...), kind=kLoop, calls=%fused_computation.195 | loop fusion | flops 25133056 | bytes 17125376 | tf_op jit(solution)/shard_map/reduce_sum | solution.py:56
  88.5 4.6 %multiply_reduce_fusion.40 = (f32[4096]{0:T(1024)}, f32[4096]{0:T(1024)}, f32[4096]{0:T(1024)}, f32[4096]{0:T(1024)}, f32[4096]{0:T(1024)}, /*index=5*/f32[4096]{0:T(1024)}, f32[4096]{0:T(1024)}, f32[4096]{0:T(1024)}) fusion(f32[128,4096]{1,0:T(8,128)S(1)} %get-tuple-element.207, f32[128,4096]{1,0:T(8,128)S(1)} %get-tuple-element.206, ...), kind=kLoop, calls=%fused_computation.203 | loop fusion | flops 16744448 | bytes 4460544 | tf_op jit(solution)/shard_map/reduce_sum | solution.py:56
  93.1 3.4 stack.169
  101.4 44.3 %all-gather.7.cloned.1.call-done = f32[128,4096]{1,0:T(8,128)} async-done(((f32[16,4096]{1,0:T(8,128)}), f32[128,4096]{1,0:T(8,128)}) %all-gather.7.cloned.1.call-update) | async-done | bytes 2097168 | tf_op jit(solution)/shard_map/all_gather | solution.py:17
  145.6 49.8 %all-gather.5.cloned.1.call-done = f32[128,4096]{1,0:T(8,128)} async-done(((f32[16,4096]{1,0:T(8,128)}), f32[128,4096]{1,0:T(8,128)}) %all-gather.5.cloned.1.call-update) | async-done | bytes 2097168 | tf_op jit(solution)/shard_map/all_gather | solution.py:17
  195.7 109.5 %while.27 = (s32[]{:T(128)}, f32[16,4096]{1,0:T(8,128)S(1)}, f32[8,16,4096]{2,1,0:T(8,128)}, f32[8,16,16]{2,1,0:T(8,128)}, f32[8,16,4096]{2,1,0:T(8,128)}, /*ind...) while((s32[]{:T(128)}, f32[16,4096]{1,0:T(8,128)S(1)}, ...), condition=%wide.region_54.55_spmd, body=%wide.region_21.54_spmd.sunk | while | flops 10485521 | bytes 10244477 | solution.py:47
  195.7 3.3 constant_dynamic-slice_fusion.81
  209.1 3.5 constant_dynamic-slice_fusion.81
  222.7 3.6 constant_dynamic-slice_fusion.81
  236.6 3.7 constant_dynamic-slice_fusion.81
  250.5 3.7 constant_dynamic-slice_fusion.81
  264.3 3.4 constant_dynamic-slice_fusion.81
  277.8 3.4 constant_dynamic-slice_fusion.81
  291.4 3.6 constant_dynamic-slice_fusion.81
  295.2 2.5 fusion.69
  305.2 11.2 %psum.15 = bf16[128,16]{1,0:T(8,128)(2,1)S(1)} all-reduce(f32[128,16]{1,0:T(8,128)} %bitcast.509), channel_id=1, replica_groups=mesh['seq'=8,'tp'=4] {'tp'}, use_global_device_ids=true, to_apply=%region_55.56 | all-reduce | flops 2048 | bytes 12288 | tf_op jit(solution)/shard_map/psum | solution.py:112
  318.7 4.0 %fusion.49 = bf16[128,4096]{1,0:T(8,128)(2,1)} fusion(f32[8,16,4096]{2,1,0:T(8,128)} %get-tuple-element.100, f32[4096]{0:T(1024)} %param.20, f32[131,4096]{1,0:T(8,128)S(1)} %maximum_convert_fusion, f32[4096]{0:T(1024)S(1)} %bitcast.503, f32[4096]{0:T(1024)S(1)} %bitcast.506, f32[4096]{0:T(1024)S(1)} %bitcast.500, f32[4096]{0:T(1024)S(1)} %bitcast.497, ...), kind=kLoop, calls=%fused_computation.185 | loop fusion | flops 8912896 | bytes 11632640 | tf_op jit(solution)/shard_map/convert_element_type | solution.py:111
  322.7 65.4 %reduce-scatter.2.cloned.1.call-done = f32[512,16]{0,1:T(8,128)} async-done(((f32[4096,16]{0,1:T(8,128)}), f32[512,16]{0,1:T(8,128)}) %reduce-scatter.2.cloned.1.call-update) | async-done | bytes 32784 | tf_op jit(solution)/shard_map/reduce_scatter | solution.py:113
  (168 shorter events, 95.8 us)
Async XLA Ops:
  7.2 11.0 %copy-start.10 = (f32[4096]{0:T(1024)S(1)}, f32[4096]{0:T(1024)}, u32[]{:S(2)}) copy-start(f32[4096]{0:T(1024)} %param.15) | copy-start | bytes 49156
  7.2 138.5 %all-gather.7.cloned.1.call-start = ((), (), s32[]{:S(2)}) async-start(), calls=%async_computation.3 | async-start | bytes 2359296 | tf_op jit(solution)/shard_map/all_gather | solution.py:17
  8.1 8.4 %collective-permute-start = (bf16[3,4096]{1,0:T(4,128)(2,1)S(1)}, bf16[3,4096]{1,0:T(4,128)(2,1)S(1)}, u32[]{:S(2)}, u32[]{:S(2)}) collective-permute-start(bf16[3,4096]{1,0:T(4,128)(2,1)S(1)} %slice.453), channel_id=1, source_target_pairs={{0,4},{4,8},{8,12},{12,16},{16,20},{20,24},{24,28},{1,5},{5,9},{9,... | collective-permute-start | bytes 73736 | tf_op jit(solution)/shard_map/ppermute | solution.py:12
  16.5 64.3 %copy-start.4 = (f32[1,4096]{1,0:T(1,128)}, f32[1,4096]{1,0:T(1,128)S(1)}, u32[]{:S(2)}) copy-start(f32[1,4096]{1,0:T(1,128)S(1)} %get-tuple-element.339) | copy-start | bytes 49156
  16.5 64.3 %copy-start.6 = (f32[1,4096]{1,0:T(1,128)}, f32[1,4096]{1,0:T(1,128)S(1)}, u32[]{:S(2)}) copy-start(f32[1,4096]{1,0:T(1,128)S(1)} %get-tuple-element.340) | copy-start | bytes 49156
  16.5 64.3 %copy-start.8 = (f32[1,4096]{1,0:T(1,128)}, f32[1,4096]{1,0:T(1,128)S(1)}, u32[]{:S(2)}) copy-start(f32[1,4096]{1,0:T(1,128)S(1)} %get-tuple-element.341) | copy-start | bytes 49156
  16.5 4.0 %slice-start = ((s8[4456448]{0:T(1024)(128)(4,1)}), s8[4194304]{0:T(1024)(128)(4,1)S(1)}, s32[]{:S(2)}) async-start(s8[4456448]{0:T(1024)(128)(4,1)} %bitcast.411), calls=%async_computation.4 | async-start | bytes 8388608
  20.5 16.4 %copy-start.14 = (f32[4096]{0:T(1024)S(1)}, f32[4096]{0:T(1024)}, u32[]{:S(2)}) copy-start(f32[4096]{0:T(1024)} %param.18) | copy-start | bytes 49156
  37.0 6.0 %copy-start.12 = (f32[128,16]{0,1:T(8,128)}, f32[128,16]{0,1:T(8,128)S(1)}, u32[]{:S(2)}) copy-start(f32[128,16]{0,1:T(8,128)S(1)} %get-tuple-element.337) | copy-start | bytes 24580
  88.5 4.6 %copy-start.2 = (f32[128,4096]{1,0:T(8,128)}, f32[128,4096]{1,0:T(8,128)S(1)}, u32[]{:S(2)}) copy-start(f32[128,4096]{1,0:T(8,128)S(1)} %get-tuple-element.207) | copy-start | bytes 6291460
  88.5 8.1 %copy-start = (f32[16,4096]{1,0:T(8,128)S(1)}, f32[16,4096]{1,0:T(8,128)}, u32[]{:S(2)}) copy-start(f32[16,4096]{1,0:T(8,128)} %param.19) | copy-start | bytes 786436
  93.1 5.1 %copy-start.3 = (bf16[128,4096]{1,0:T(8,128)(2,1)S(1)}, bf16[128,4096]{1,0:T(8,128)(2,1)}, u32[]{:S(2)}) copy-start(bf16[128,4096]{1,0:T(8,128)(2,1)} %param.21) | copy-start | bytes 3145732
  96.6 98.8 %all-gather.5.cloned.1.call-start = ((), (), s32[]{:S(2)}) async-start(), calls=%async_computation.2 | async-start | bytes 2359296 | tf_op jit(solution)/shard_map/all_gather | solution.py:17
  98.1 290.0 %reduce-scatter.2.cloned.1.call-start = ((), (), s32[]{:S(2)}) async-start(), calls=%async_computation.1 | async-start | bytes 294912 | tf_op jit(solution)/shard_map/reduce_scatter | solution.py:113
  195.7 123.0 %copy-start.5 = (f32[1,4096]{1,0:T(1,128)S(1)}, f32[1,4096]{1,0:T(1,128)}, u32[]{:S(2)}) copy-start(f32[1,4096]{1,0:T(1,128)} %copy-done.4) | copy-start | bytes 49156
  195.7 123.0 %copy-start.7 = (f32[1,4096]{1,0:T(1,128)S(1)}, f32[1,4096]{1,0:T(1,128)}, u32[]{:S(2)}) copy-start(f32[1,4096]{1,0:T(1,128)} %copy-done.6) | copy-start | bytes 49156
  195.7 123.0 %copy-start.9 = (f32[1,4096]{1,0:T(1,128)S(1)}, f32[1,4096]{1,0:T(1,128)}, u32[]{:S(2)}) copy-start(f32[1,4096]{1,0:T(1,128)} %copy-done.8) | copy-start | bytes 49156
  195.7 123.0 %copy-start.11 = (f32[4096]{0:T(1024)S(1)}, f32[4096]{0:T(1024)}, u32[]{:S(2)}) copy-start(f32[4096]{0:T(1024)} %param.15) | copy-start | bytes 49156
  203.6 3.0 copy-start.13
  217.3 3.0 copy-start.13
  231.1 3.0 copy-start.13
  245.0 3.0 copy-start.13
  285.9 3.0 copy-start.13
  299.7 3.0 copy-start.13
  (4 other events, 9.3 us)
Sparse Core Ops, SparseCore 0:
  96.7 48.8 all-gather.6
  147.8 47.6 all-gather.4
  318.8 69.2 reduce-scatter.1
where the time goes:
time: 398 us; the launch traced here: 395 us
  waiting for transfers between devices  159 us (40%)
  local copies, waits for them, and re-layouts  90.4 us (23%)
  other arithmetic  89.8 us (23%)
  blocking collectives  25.7 us (6%)
  between operations  14 us (4%)
  matrix products  9.51 us (2%)
  starting transfers between devices  4.99 us (1%)
    all_gather x2, waiting for transfers between devices, entering(): gathered = jax.tree.map(lambda a: lax.all_gather(a, axis), part)  94 us
    reduce_scatter x1, waiting for transfers between devices, on_device(): lax.psum_scatter(lax.dot_general(conv_out, grad_c, (((0,), (0,)), ((), ()...  65.4 us
    reduce_sum x40, other arithmetic, block_step(): grads.append(jnp.sum(carried * grad_now[offset][None, :], axis=1))  39.7 us
    rev x2, local copies, waits for them, and re-layouts, local_ending(): after = jnp.flip(jnp.cumsum(jnp.flip(step_size, 0), axis=0), 0) - step_size  33.2 us
    slice x8, local copies, waits for them, and re-layouts, block_step(): grads.append(jnp.sum(carried * grad_now[offset][None, :], axis=1))  28.2 us
    neg x8, other arithmetic, block_step(): -step_now[offset][None, :] * decay_rate  20 us
    psum x1, blocking collectives, on_device(): proj_out = lax.psum(partial_proj, 'tp').astype(jnp.bfloat16)  14.5 us
    reduce_sum x2, other arithmetic, local_ending(): jnp.sum(weights * drive_in * b_matrix[:, state_index:state_index + 1], ax...  12.3 us
  transfers between devices with their start and end apart: 4, of which 3 were waited for; matrix products, arithmetic and copies ran while one was open for 3% of the time, Pallas kernels for 0%

commit v1 on v0

--- a/solution.py
+++ b/solution.py
@@ -4,6 +4,11 @@
 from jax.sharding import PartitionSpec as P
 
 block_len = 16
+
+
+def guide_node_on_mesh(raw):
+    part_now = lax.all_gather(raw, "tp").sum(axis=0)
+    return part_now
 
 
 def shifted(shard, axis, by):
@@ -83,7 +88,7 @@
         )
     conv_out = jax.nn.silu(pre_act).astype(jnp.bfloat16)
     partial_proj = jnp.dot(conv_out, proj_weight, preferred_element_type=jnp.float32)
-    proj_out = lax.psum(partial_proj, "tp").astype(jnp.bfloat16)
+    proj_out = guide_node_on_mesh(partial_proj).astype(jnp.bfloat16)
     dt_low = proj_out[:, :rank_width]
     b_matrix = proj_out[:, rank_width : rank_width + states].astype(jnp.float32)
     c_matrix = proj_out[:, rank_width + states :].astype(jnp.float32)

time: 398 us -> 414 us (1.040)
  waiting for transfers between devices: 159 us -> 180 us
  blocking collectives: 25.7 us -> 10.7 us
  other arithmetic: 89.8 us -> 99.8 us
    all_gather x0 -> x1, waiting for transfers between devices: none -> 18.9 us  [guide_node_on_mesh(): part_now = lax.all_gather(raw, 'tp').sum(axis=0)]
    psum x1 -> x0, blocking collectives: 14.5 us -> none  [on_device(): proj_out = lax.psum(partial_proj, 'tp').astype(jnp.bfloat16)]
    reduce_sum x40, other arithmetic: 39.7 us -> 51.3 us  [block_step(): grads.append(jnp.sum(carried * grad_now[offset][None, :], axis=1))]
    another operation x16, local copies, waits for them, and re-layouts: 8.92 us -> 14.6 us  [block_step(): return (carried, (jnp.stack(outputs), jnp.stack(grads)))]
    dynamic_update_slice x16, local copies, waits for them, and re-layouts: 10.6 us -> 5.86 us  [local_pass(): return lax.scan(block_step, initial, slices)]
  transfers between devices with their start and end apart: 4 -> 5, of which waited for: 3 -> 5; matrix products, arithmetic and copies ran while one was open for 3% -> 2% of each run, Pallas kernels for 0% -> 0%
where the time goes in v1:
time: 414 us; the launch traced here: 411 us
  waiting for transfers between devices  180 us (43%)
  other arithmetic  99.8 us (24%)
  local copies, waits for them, and re-layouts  90.8 us (22%)
  between operations  14 us (3%)
  blocking collectives  10.7 us (3%)
  matrix products  9.62 us (2%)
  starting transfers between devices  5.22 us (1%)
    all_gather x2, waiting for transfers between devices, entering(): gathered = jax.tree.map(lambda a: lax.all_gather(a, axis), part)  95.1 us
    reduce_scatter x1, waiting for transfers between devices, on_device(): lax.psum_scatter(lax.dot_general(conv_out, grad_c, (((0,), (0,)), ((), ()...  65.3 us
    reduce_sum x40, other arithmetic, block_step(): grads.append(jnp.sum(carried * grad_now[offset][None, :], axis=1))  51.3 us
    rev x2, local copies, waits for them, and re-layouts, local_ending(): after = jnp.flip(jnp.cumsum(jnp.flip(step_size, 0), axis=0), 0) - step_size  33.3 us
    slice x8, local copies, waits for them, and re-layouts, block_step(): grads.append(jnp.sum(carried * grad_now[offset][None, :], axis=1))  28.2 us
    neg x8, other arithmetic, block_step(): -step_now[offset][None, :] * decay_rate  20 us
    all_gather x1, waiting for transfers between devices, guide_node_on_mesh(): part_now = lax.all_gather(raw, 'tp').sum(axis=0)  18.9 us
    another operation x16, local copies, waits for them, and re-layouts, block_step(): return (carried, (jnp.stack(outputs), jnp.stack(grads)))  14.6 us
  transfers between devices with their start and end apart: 5, of which 5 were waited for; matrix products, arithmetic and copies ran while one was open for 2% of the time, Pallas kernels for 0%

profile of v1, /device:TPU:0, one launch (start us, length us, event | category | flops | bytes accessed | tf_op | source)
XLA Modules:
  0.0 410.7 jit_solution(11681784516430478369)
XLA Ops:
  8.1 4.9 %collective-permute-start = (bf16[3,4096]{1,0:T(4,128)(2,1)S(1)}, bf16[3,4096]{1,0:T(4,128)(2,1)S(1)}, u32[]{:S(2)}, u32[]{:S(2)}) collective-permute-start(bf16[3,4096]{1,0:T(4,128)(2,1)S(1)} %slice.453), channel_id=1, source_target_pairs={{0,4},{4,8},{8,12},{12,16},{16,20},{20,24},{24,28},{1,5},{5,9},{9,... | collective-permute-start | bytes 73736 | tf_op jit(solution)/shard_map/ppermute | solution.py:17
  21.2 18.9 %all-gather.7.cloned.1.call-done = f32[512,544]{0,1:T(8,128)} async-done(((f32[128,544]{0,1:T(8,128)}), f32[512,544]{0,1:T(8,128)}) %all-gather.7.cloned.1.call-update) | async-done | bytes 1114128 | tf_op jit(solution)/shard_map/all_gather | solution.py:10
  40.0 2.6 reshape.346
  44.6 5.4 %fusion.58 = (f32[4096]{0:T(1024)S(1)}, f32[128,4096]{1,0:T(8,128)}) fusion(f32[4096]{0:T(1024)S(1)} %copy-done.4, bf16[512,4096]{1,0:T(8,128)(2,1)} %param.17, bf16[128,544]{0,1:T(8,128)(2,1)S(1)} %reduce_sum.450), kind=kOutput, calls=%fused_computation.252 | convolution fusion | flops 541061120 | bytes 6455296 | tf_op jit(solution)/shard_map/dot_general | solution.py:96
  50.0 16.6 %rev.7 = f32[128,4096]{1,0:T(8,128)} reverse(f32[128,4096]{1,0:T(8,128)} %get-tuple-element.349), dimensions={0} | reverse | bytes 4194304 | tf_op jit(solution)/shard_map/jit(_flip)/rev | solution.py:56
  66.6 4.6 %reduce_window_sum.11 = f32[128,4096]{1,0:T(8,128)} reduce-window(f32[128,4096]{1,0:T(8,128)} %rev.7, f32[]{:T(128)} %constant.51.clone.1), window={size=128x1 pad=127_0x0_0}, to_apply=%region_2.3 | reduce-window | flops 66584576 | bytes 4194308 | tf_op jit(solution)/shard_map/jit(cumsum)/reduce_window_sum | solution.py:56
  71.3 16.6 %rev.8 = f32[128,4096]{1,0:T(8,128)} reverse(f32[128,4096]{1,0:T(8,128)} %reduce_window_sum.11), dimensions={0} | reverse | bytes 4194304 | tf_op jit(solution)/shard_map/jit(_flip)/rev | solution.py:56
  87.9 7.0 %multiply_reduce_fusion.32 = (f32[4096]{0:T(1024)S(1)}, f32[4096]{0:T(1024)S(1)}, f32[4096]{0:T(1024)S(1)}, f32[4096]{0:T(1024)S(1)}, f32[4096]{0:T(1024)S(1)}, ...) fusion(f32[128]{0:T(128)S(1)} %get-tuple-element.333, ...), kind=kLoop, calls=%fused_computation.195 | loop fusion | flops 25133056 | bytes 17125376 | tf_op jit(solution)/shard_map/reduce_sum | solution.py:61
  95.0 4.0 multiply_reduce_fusion.40
  101.6 2.8 convert_multiply_fusion.2
  104.6 45.4 %all-gather.11.cloned.1.call-done = f32[128,4096]{1,0:T(8,128)} async-done(((f32[16,4096]{1,0:T(8,128)}), f32[128,4096]{1,0:T(8,128)}) %all-gather.11.cloned.1.call-update) | async-done | bytes 2097168 | tf_op jit(solution)/shard_map/all_gather | solution.py:22
  149.9 49.8 %all-gather.9.cloned.1.call-done = f32[128,4096]{1,0:T(8,128)} async-done(((f32[16,4096]{1,0:T(8,128)}), f32[128,4096]{1,0:T(8,128)}) %all-gather.9.cloned.1.call-update) | async-done | bytes 2097168 | tf_op jit(solution)/shard_map/all_gather | solution.py:22
  200.0 121.9 %while.27 = (s32[]{:T(128)}, f32[16,4096]{1,0:T(8,128)S(1)}, f32[8,16,4096]{2,1,0:T(8,128)}, f32[8,16,16]{2,1,0:T(8,128)S(1)}, f32[8,16,4096]{2,1,0:T(8,128)}, /...) while((s32[]{:T(128)}, f32[16,4096]{1,0:T(8,128)S(1)}, ...), condition=%wide.region_54.55_spmd, body=%wide.region_21.54_spmd.sunk | while | flops 10485521 | bytes 10250853 | solution.py:52
  200.0 3.3 constant_dynamic-slice_fusion.81
  214.9 3.5 constant_dynamic-slice_fusion.81
  230.1 3.6 constant_dynamic-slice_fusion.81
  245.5 3.7 constant_dynamic-slice_fusion.81
  260.9 3.7 constant_dynamic-slice_fusion.81
  276.3 3.4 constant_dynamic-slice_fusion.81
  291.4 3.4 constant_dynamic-slice_fusion.81
  306.5 3.6 constant_dynamic-slice_fusion.81
  321.9 10.7 %psum.7 = bf16[128,16]{1,0:T(8,128)(2,1)S(1)} all-reduce(f32[128,16]{1,0:T(8,128)S(1)} %bitcast.511), channel_id=1, replica_groups=mesh['seq'=8,'tp'=4] {'tp'}, use_global_device_ids=true, to_apply=%region_55.56 | all-reduce | flops 2048 | bytes 12288 | tf_op jit(solution)/shard_map/psum | solution.py:117
  334.8 4.0 fusion.49
  338.8 65.3 %reduce-scatter.2.cloned.1.call-done = f32[512,16]{0,1:T(8,128)} async-done(((f32[4096,16]{0,1:T(8,128)}), f32[512,16]{0,1:T(8,128)}) %reduce-scatter.2.cloned.1.call-update) | async-done | bytes 32784 | tf_op jit(solution)/shard_map/reduce_scatter | solution.py:118
  (138 shorter events, 109.4 us)
Async XLA Ops:
  7.2 9.1 %copy-start.3 = (f32[4096]{0:T(1024)S(1)}, f32[4096]{0:T(1024)}, u32[]{:S(2)}) copy-start(f32[4096]{0:T(1024)} %param.15) | copy-start | bytes 49156
  7.2 32.9 %all-gather.7.cloned.1.call-start = ((), (), s32[]{:S(2)}) async-start(), calls=%async_computation.2 | async-start | bytes 1392640 | tf_op jit(solution)/shard_map/all_gather | solution.py:10
  8.1 6.5 %collective-permute-start = (bf16[3,4096]{1,0:T(4,128)(2,1)S(1)}, bf16[3,4096]{1,0:T(4,128)(2,1)S(1)}, u32[]{:S(2)}, u32[]{:S(2)}) collective-permute-start(bf16[3,4096]{1,0:T(4,128)(2,1)S(1)} %slice.453), channel_id=1, source_target_pairs={{0,4},{4,8},{8,12},{12,16},{16,20},{20,24},{24,28},{1,5},{5,9},{9,... | collective-permute-start | bytes 73736 | tf_op jit(solution)/shard_map/ppermute | solution.py:17
  14.5 4.0 slice-start
  16.2 2.3 slice-start.1
  17.6 1.0 copy-start.1
  18.6 2.3 copy-start
  20.6 24.0 %copy-start.4 = (f32[4096]{0:T(1024)S(1)}, f32[4096]{0:T(1024)}, u32[]{:S(2)}) copy-start(f32[4096]{0:T(1024)} %param.18) | copy-start | bytes 49156
  20.6 129.3 %all-gather.11.cloned.1.call-start = ((), (), s32[]{:S(2)}) async-start(), calls=%async_computation.4 | async-start | bytes 2359296 | tf_op jit(solution)/shard_map/all_gather | solution.py:22
  95.0 4.0 copy-start.2
  100.7 99.0 %all-gather.9.cloned.1.call-start = ((), (), s32[]{:S(2)}) async-start(), calls=%async_computation.3 | async-start | bytes 2359296 | tf_op jit(solution)/shard_map/all_gather | solution.py:22
  101.5 302.6 %reduce-scatter.2.cloned.1.call-start = ((), (), s32[]{:S(2)}) async-start(), calls=%async_computation.1 | async-start | bytes 294912 | tf_op jit(solution)/shard_map/reduce_scatter | solution.py:118
Sparse Core Ops, SparseCore 0:
  20.7 19.2 all-gather.6
  100.8 49.0 all-gather.10
  152.1 47.6 all-gather.8
  334.9 69.1 reduce-scatter.1
